TPU v7x, 512 devices: a whole 4x8x8 slice. The times are simulated.
512 devices in a mesh: gx: 32 (over y, x), gy: 16 (over z, core).
Axes of the slice: x: 4, y: 8, z: 8, core: 2. Of those that a mesh axis runs over, the one named last changes fastest.
Arguments:
- source: float32 [512, 256, 128], P('gx', 'gy'), may hold values from -8 to 8
- diffuse_first: float32 [512, 256, 128], P('gx', 'gy'), may hold values from 0.5 to 8
- diffuse_second: float32 [512, 256, 128], P('gx', 'gy'), may hold values from 0.5 to 8
- diffuse_third: float32 [512, 256, 128], P('gx', 'gy'), may hold values from 0.5 to 8
- reaction: float32 [512, 256, 128], P('gx', 'gy'), may hold values from 0.005 to 0.05
- deflation: float32 [8, 512, 256, 128], P(None, 'gx', 'gy'), may hold values from -1.5 to 1.5
Outputs:
- iterate: float32 [512, 256, 128], P('gx', 'gy')
- residual: float32 [512, 256, 128], P('gx', 'gy')
All inputs are finite; a program needn't handle non-finite values.
Results may differ from a plain program's by a relative error of at most 0.0003.
Values sent between devices are 32-bit elements; how exact they have to be, the bound alone decides.
A program may use at most 64 MiB of HBM per device.

v0:
```python
import jax
import jax.numpy as jnp
from jax import lax
from jax.sharding import PartitionSpec as P

LEVELS = 3
COARSE_SWEEPS = 3
ITERS = 2


RELAX_WEIGHT = 0.6
TOP_PRECISION = lax.Precision.HIGHEST


def extended(cells, sides, width):
    for axis, dim in sides:
        count = lax.axis_size(axis)
        ends = count - 1
        head = lax.slice_in_dim(cells, 0, width, axis=dim)
        tail = lax.slice_in_dim(cells, cells.shape[dim] - width, cells.shape[dim], axis=dim)
        cells = jnp.concatenate(
            [
                lax.ppermute(tail, axis, [(i, (i + 1) % count) for i in range(ends)]),
                cells,
                lax.ppermute(head, axis, [((i + 1) % count, i) for i in range(ends)]),
            ],
            axis=dim,
        )
    return cells


def passed_along(block, axis, distance):
    devices = range(lax.axis_size(axis))
    route = [(i - distance, i) for i in devices if i - distance in devices]
    return lax.ppermute(block, axis, route)


def shift_lower(values, which):
    which = which % values.ndim
    count = values.shape[which]
    zero = jnp.zeros_like(lax.slice_in_dim(values, 0, 1, axis=which))
    return jnp.concatenate([zero, lax.slice_in_dim(values, 0, count - 1, axis=which)], axis=which)


def shift_upper(values, which):
    which = which % values.ndim
    count = values.shape[which]
    zero = jnp.zeros_like(lax.slice_in_dim(values, 0, 1, axis=which))
    return jnp.concatenate([lax.slice_in_dim(values, 1, count, axis=which), zero], axis=which)


def fold_pairs(values, which):
    shape = values.shape
    new_shape = shape[:which] + (shape[which] // 2, 2) + shape[which + 1 :]
    return values.reshape(new_shape).sum(axis=which + 1)


def fold_blocks(values, which_dims):
    for which in which_dims:
        values = fold_pairs(values, which)
    return values


def make_level(face_first, lower_first, face_second, lower_second, face_third, lower_third, react):
    diag = react + face_first + lower_first + face_second + lower_second + face_third + lower_third
    return (
        face_first,
        lower_first,
        face_second,
        lower_second,
        face_third,
        lower_third,
        react,
        diag,
        1.0 / diag,
    )


def coarsen(level):
    (
        face_first,
        lower_first,
        face_second,
        lower_second,
        face_third,
        lower_third,
        react,
        diag,
        inverse,
    ) = level
    return make_level(
        fold_blocks(face_first[1::2], (1, 2)),
        fold_blocks(lower_first[0::2], (1, 2)),
        fold_blocks(face_second[:, 1::2], (0, 2)),
        fold_blocks(lower_second[:, 0::2], (0, 2)),
        fold_blocks(face_third[:, :, 1::2], (0, 1)),
        fold_blocks(lower_third[:, :, 0::2], (0, 1)),
        fold_blocks(react, (0, 1, 2)),
    )


def operate_padded(padded, field, level):
    (
        face_first,
        lower_first,
        face_second,
        lower_second,
        face_third,
        lower_third,
        react,
        diag,
        inverse,
    ) = level
    return (
        diag * field
        - face_first * padded[..., 2:, 1:-1, :]
        - lower_first * padded[..., :-2, 1:-1, :]
        - face_second * padded[..., 1:-1, 2:, :]
        - lower_second * padded[..., 1:-1, :-2, :]
        - face_third * shift_upper(field, -1)
        - lower_third * shift_lower(field, -1)
    )


def operate(field, level):
    padded = extended(field, (("gx", 1), ("gy", 2)), 1)
    return operate_padded(padded, field, level)


def prolong(coarse):
    return jnp.repeat(jnp.repeat(jnp.repeat(coarse, 2, 1), 2, 2), 2, 3)


def coarsest_solve(right, level):
    inverse = level[8]
    field = RELAX_WEIGHT * right * inverse
    for sweep in range(COARSE_SWEEPS - 1):
        field = field + RELAX_WEIGHT * (right - operate(field, level)) * inverse
    return field


def vee_cycle(right, levels, margin_level, level_index):
    level = levels[level_index]
    if level_index == len(levels) - 1:
        return coarsest_solve(right, level)
    inverse = level[8]
    field = RELAX_WEIGHT * right * inverse
    defect = right - operate(field, level)
    field = field + prolong(
        vee_cycle(fold_blocks(defect, (1, 2, 3)), levels, margin_level, level_index + 1)
    )
    return field + RELAX_WEIGHT * (right - operate(field, level)) * inverse


def small_solve(factor, values):
    count = factor.shape[0]
    forward = []
    for place in range(count):
        value = values[place]
        for other in range(place):
            value = value - factor[place, other] * forward[other]
        forward.append(value / factor[place, place])
    backward = [None] * count
    for place in range(count - 1, -1, -1):
        value = forward[place]
        for other in range(place + 1, count):
            value = value - factor[other, place] * backward[other]
        backward[place] = value / factor[place, place]
    return jnp.stack(backward)


def project(vectors, field):
    return jnp.einsum("kxyz,xyz->k", vectors, field, precision=TOP_PRECISION)


def expand(vectors, weights):
    return jnp.einsum("k,kxyz->xyz", weights, vectors, precision=TOP_PRECISION)


def deflation_sums(residual, precond, images):
    return lax.psum((jnp.sum(residual * precond), project(images, precond)), ("gx", "gy"))


def per_device(source, diffuse_first, diffuse_second, diffuse_third, reaction, deflation):
    first_cells, second_cells, third_cells = source.shape
    first_index = lax.axis_index("gx") * first_cells + lax.broadcasted_iota(
        jnp.int32, source.shape, 0
    )
    second_index = lax.axis_index("gy") * second_cells + lax.broadcasted_iota(
        jnp.int32, source.shape, 1
    )
    third_index = lax.broadcasted_iota(jnp.int32, source.shape, 2)
    face_first = diffuse_first * (first_index < lax.axis_size("gx") * first_cells - 1).astype(
        jnp.float32
    )
    face_second = diffuse_second * (second_index < lax.axis_size("gy") * second_cells - 1).astype(
        jnp.float32
    )
    face_third = diffuse_third * (third_index < third_cells - 1).astype(jnp.float32)
    first_rim = passed_along(face_first[-1:], "gx", 1)
    second_rim = passed_along(face_second[:, -1:], "gy", 1)
    lower_first = jnp.concatenate([first_rim, face_first[:-1]], axis=0)
    lower_second = jnp.concatenate([second_rim, face_second[:, :-1]], axis=1)
    basis_padded = extended(deflation, (("gx", 1), ("gy", 2)), 1)
    level = make_level(
        face_first,
        lower_first,
        face_second,
        lower_second,
        face_third,
        shift_lower(face_third, 2),
        reaction,
    )
    levels = [level]
    for level_index in range(LEVELS - 1):
        levels.append(coarsen(levels[-1]))
    margin_level = None

    def precondition(vector):
        return vee_cycle(vector[None], levels, margin_level, 0)[0]

    images = operate_padded(basis_padded, deflation, level)
    local_matrix = jnp.einsum("kxyz,mxyz->km", deflation, images, precision=TOP_PRECISION)
    matrix, source_proj = lax.psum((local_matrix, project(deflation, source)), ("gx", "gy"))
    matrix = 0.5 * (matrix + matrix.T)
    factor = jnp.linalg.cholesky(matrix)
    start_weights = small_solve(factor, source_proj)
    iterate = expand(deflation, start_weights)
    residual = source - expand(images, start_weights)
    precond = precondition(residual)
    inner_now, projected = deflation_sums(residual, precond, images)
    weights = small_solve(factor, projected)
    search = precond - expand(deflation, weights)
    for turn in range(ITERS):
        image = operate(search[None], level)[0]
        alpha = inner_now / lax.psum(jnp.sum(search * image), ("gx", "gy"))
        iterate = iterate + alpha * search
        residual = residual - alpha * image
        if turn + 1 < ITERS:
            precond = precondition(residual)
            inner_next, projected = deflation_sums(residual, precond, images)
            weights = small_solve(factor, projected)
            search = precond + inner_next / inner_now * search - expand(deflation, weights)
            inner_now = inner_next
    return (iterate, residual)


def solution(mesh):
    return jax.shard_map(
        per_device,
        mesh=mesh,
        in_specs=(
            P("gx", "gy", None),
            P("gx", "gy", None),
            P("gx", "gy", None),
            P("gx", "gy", None),
            P("gx", "gy", None),
            P(None, "gx", "gy", None),
        ),
        out_specs=(P("gx", "gy", None), P("gx", "gy", None)),
        check_vma=False,
    )
```

profile of v0, /device:TPU:27, one launch (start us, length us, event | category | flops | bytes accessed | tf_op | source)
XLA Modules:
  0.0 1080.7 jit_solution(12904635899617955407)
XLA Ops:
  2.3 4.5 collective-permute-start.1
  8.5 3.1 collective-permute-start
  14.1 2.8 collective-permute-start.3
  16.9 2.5 collective-permute-start.2
  21.2 3.1 convolution_bitcast_fusion.3
  31.2 2.9 slice.1000
  46.6 2.3 slice.1001
  60.5 3.8 collective-permute-start.5
  65.6 2.3 fusion.3
  67.9 2.5 convolution_bitcast_fusion
  70.5 104.8 %all-reduce.33 = (f32[8]{0:T(128)S(1)}, f32[8,8]{0,1:T(8,128)S(1)}) all-reduce(f32[8]{0:T(128)S(1)} %copy-done.73, f32[8,8]{0,1:T(8,128)S(1)} %convolution_bitcast_fusion), channel_id=1, replica_groups=mesh['gx'=32,'gy'=16] {'gx','gy'}, use_global_device_ids=true, to_apply=%region_0.0 | all-reduce | flops 72 | bytes 576 | tf_op jit(solution)/shard_map/psum | solution.py:224
  232.6 2.1 collective-permute-start.6
  234.6 3.4 collective-permute-start.7
  241.8 3.1 collective-permute-start.8
  244.9 2.7 collective-permute-start.9
  257.0 3.7 collective-permute-start.10
  263.4 2.4 slice.1013
  270.4 2.3 collective-permute-start.12
  272.8 4.0 collective-permute-start.13
  286.2 4.0 collective-permute-start.14
  290.2 2.2 collective-permute-start.15
  292.5 4.6 collective-permute-done.15
  299.2 5.2 collective-permute-start.17
  306.1 5.8 collective-permute-start.18
  313.8 2.5 collective-permute-done.19
  318.4 5.7 collective-permute-start.21
  335.1 3.8 collective-permute-start.22
  340.8 2.4 collective-permute-done.23
  345.2 5.7 collective-permute-start.25
  352.9 2.1 broadcast_in_dim.89
  356.8 3.8 collective-permute-start.26
  362.5 2.5 collective-permute-done.27
  366.9 5.8 collective-permute-start.29
  375.1 2.4 convolution_bitcast_fusion.2
  377.5 111.7 %psum.59 = f32[8]{0:T(128)S(1)} all-reduce(f32[8]{0:T(128)S(1)} %convolution_bitcast_fusion.2), channel_id=1, replica_groups=mesh['gx'=32,'gy'=16] {'gx','gy'}, use_global_device_ids=true, to_apply=%region_42.43 | all-reduce | flops 8 | bytes 64 | tf_op jit(solution)/shard_map/psum | solution.py:181
  543.1 3.4 collective-permute-start.31
  547.5 3.7 collective-permute-start.32
  556.0 103.2 %all-reduce.32 = (f32[]{:T(128)}, f32[]{:T(128)}) all-reduce(f32[]{:T(128)} %get-tuple-element.36, f32[]{:T(128)} %get-tuple-element.34), channel_id=1, replica_groups=mesh['gx'=32,'gy'=16] {'gx','gy'}, use_global_device_ids=true, to_apply=%region_41.42 | all-reduce | flops 2 | bytes 16 | tf_op jit(solution)/shard_map/psum | solution.py:181
  663.3 3.4 collective-permute-start.35
  667.7 3.2 collective-permute-start.36
  671.0 2.3 collective-permute-start.37
  681.4 5.5 collective-permute-start.38
  688.8 2.4 collective-permute-done.39
  691.2 2.3 collective-permute-start.40
  693.6 5.2 collective-permute-start.41
  707.8 3.8 collective-permute-start.42
  713.5 2.5 collective-permute-done.43
  718.3 5.6 collective-permute-start.45
  726.6 3.8 collective-permute-start.46
  732.3 2.5 collective-permute-done.47
  736.9 5.7 collective-permute-start.49
  751.0 3.8 collective-permute-start.50
  756.7 2.4 collective-permute-done.51
  761.1 5.7 collective-permute-start.53
  769.6 2.1 broadcast_in_dim.104
  773.4 3.8 collective-permute-start.54
  779.1 2.5 collective-permute-done.55
  783.5 5.9 collective-permute-start.57
  791.7 2.4 convolution_bitcast_fusion.1
  794.1 113.4 %all-reduce.31 = (f32[8]{0:T(128)S(1)}, f32[]{:T(128)}) all-reduce(f32[8]{0:T(128)S(1)} %convolution_bitcast_fusion.1, f32[]{:T(128)} %get-tuple-element.30), channel_id=1, replica_groups=mesh['gx'=32,'gy'=16] {'gx','gy'}, use_global_device_ids=true, to_apply=%region_53.54 | all-reduce | flops 9 | bytes 72 | tf_op jit(solution)/shard_map/psum | solution.py:181
  962.7 3.4 collective-permute-start.59
  967.6 2.8 collective-permute-start.60
  970.4 2.8 collective-permute-start.61
  974.9 102.6 %psum.63 = f32[]{:T(128)} all-reduce(f32[]{:T(128)} %get-tuple-element.28), channel_id=1, replica_groups=mesh['gx'=32,'gy'=16] {'gx','gy'}, use_global_device_ids=true, to_apply=%region_55.56 | all-reduce | flops 1 | bytes 8 | tf_op jit(solution)/shard_map/psum | solution.py:236
  (438 shorter events, 182.6 us)
Async XLA Ops:
  2.3 42.4 %collective-permute-start.1 = (f32[16,1,128]{2,0,1:T(8,128)}, f32[16,1,128]{2,0,1:T(8,128)S(1)}, u32[]{:S(2)}, u32[]{:S(2)}) collective-permute-start(f32[16,1,128]{2,0,1:T(8,128)} %slice.1156), channel_id=1, source_target_pairs={{0,1},{1,2},{2,3},{3,4},{4,5},{5,6},{6,7},{7,8},{8,9},{9,10},{10,1... | collective-permute-start | bytes 24584 | tf_op jit(solution)/shard_map/ppermute | solution.py:35
  8.5 36.2 %collective-permute-start = (f32[1,16,128]{2,0,1:T(1,128)}, f32[1,16,128]{2,0,1:T(1,128)}, u32[]{:S(2)}, u32[]{:S(2)}) collective-permute-start(f32[1,16,128]{2,0,1:T(1,128)} %slice.1154), channel_id=1, source_target_pairs={{0,16},{16,32},{32,48},{48,64},{64,80},{80,96},{96,112},{112,128},... | collective-permute-start | bytes 24584 | tf_op jit(solution)/shard_map/ppermute | solution.py:35
  14.1 41.8 %collective-permute-start.3 = (f32[8,1,16,128]{3,0,2,1:T(8,128)}, f32[8,1,16,128]{3,0,2,1:T(8,128)}, u32[]{:S(2)}, u32[]{:S(2)}) collective-permute-start(f32[8,1,16,128]{3,0,2,1:T(8,128)} %get-tuple-element.51), channel_id=1, source_target_pairs={{0,16},{16,32},{32,48},{48,64},{64,80},{80,96},{96,112},{112,128},... | collective-permute-start | bytes 196616 | tf_op jit(solution)/shard_map/ppermute | solution.py:23
  16.9 40.6 %collective-permute-start.2 = (f32[8,1,16,128]{3,0,2,1:T(8,128)}, f32[8,1,16,128]{3,0,2,1:T(8,128)}, u32[]{:S(2)}, u32[]{:S(2)}) collective-permute-start(f32[8,1,16,128]{3,0,2,1:T(8,128)} %get-tuple-element.50), channel_id=1, source_target_pairs={{16,0},{32,16},{48,32},{64,48},{80,64},{96,80},{112,96},{128,112},... | collective-permute-start | bytes 196616 | tf_op jit(solution)/shard_map/ppermute | solution.py:25
  58.5 6.5 collective-permute-start.4
  60.5 5.0 collective-permute-start.5
  70.4 162.0 %copy-start.55 = (f32[16,16,128]{2,1,0:T(8,128)S(1)}, f32[16,16,128]{2,1,0:T(8,128)}, u32[]{:S(2)}) copy-start(f32[16,16,128]{2,1,0:T(8,128)} %param.6) | copy-start | bytes 393220
  232.6 9.2 collective-permute-start.6
  234.6 7.1 collective-permute-start.7
  241.8 5.9 collective-permute-start.8
  244.9 3.5 collective-permute-start.9
  257.0 12.6 %collective-permute-start.10 = (f32[1,1,8,64]{3,2,1,0:T(8,128)}, f32[1,1,8,64]{3,2,1,0:T(8,128)S(1)}, u32[]{:S(2)}, u32[]{:S(2)}) collective-permute-start(f32[1,1,8,64]{3,2,1,0:T(8,128)} %get-tuple-element.137), channel_id=1, source_target_pairs={{16,0},{32,16},{48,32},{64,48},{80,64},{96,80},{112,96},{128,112},... | collective-permute-start | bytes 6152 | tf_op jit(solution)/shard_map/ppermute | solution.py:25
  260.7 8.9 collective-permute-start.11
  270.4 7.3 collective-permute-start.12
  272.8 4.9 collective-permute-start.13
  286.2 6.3 collective-permute-start.14
  290.2 6.9 collective-permute-start.15
  297.2 7.4 collective-permute-start.16
  299.2 6.8 collective-permute-start.17
  306.1 7.7 collective-permute-start.18
  311.8 4.5 collective-permute-start.19
  316.4 8.0 collective-permute-start.20
  318.4 7.4 collective-permute-start.21
  335.1 5.7 collective-permute-start.22
  338.9 4.4 collective-permute-start.23
  343.3 7.8 collective-permute-start.24
  345.2 6.5 collective-permute-start.25
  356.8 5.7 collective-permute-start.26
  360.5 4.4 collective-permute-start.27
  364.9 7.9 collective-permute-start.28
  366.9 6.4 collective-permute-start.29
  541.2 5.3 collective-permute-start.30
  543.1 4.4 collective-permute-start.31
  547.5 5.9 collective-permute-start.32
  551.3 3.1 collective-permute-start.33
  661.4 5.3 collective-permute-start.34
  663.3 4.4 collective-permute-start.35
  667.7 5.7 collective-permute-start.36
  671.0 3.1 collective-permute-start.37
  681.4 7.4 collective-permute-start.38
  686.8 4.4 collective-permute-start.39
  691.2 7.6 collective-permute-start.40
  693.6 6.0 collective-permute-start.41
  707.8 5.7 collective-permute-start.42
  711.6 4.5 collective-permute-start.43
  716.2 8.0 collective-permute-start.44
  718.3 7.2 collective-permute-start.45
  726.6 5.7 collective-permute-start.46
  730.4 4.5 collective-permute-start.47
  735.0 8.0 collective-permute-start.48
  736.9 7.4 collective-permute-start.49
  751.0 5.7 collective-permute-start.50
  754.8 4.4 collective-permute-start.51
  759.1 7.8 collective-permute-start.52
  761.1 6.5 collective-permute-start.53
  773.4 5.7 collective-permute-start.54
  777.2 4.4 collective-permute-start.55
  781.6 7.9 collective-permute-start.56
  783.5 6.4 collective-permute-start.57
  794.1 172.0 %copy-start.72 = (f32[8]{0:T(128)S(1)}, f32[8]{0:T(128)}, u32[]{:S(2)}) copy-start(f32[8]{0:T(128)} %copy-done.71) | copy-start | bytes 100
  960.8 6.8 collective-permute-start.58
  962.7 4.9 collective-permute-start.59
  967.6 5.7 collective-permute-start.60
  970.4 3.6 collective-permute-start.61
  (72 other events, 1213.4 us)
where the time goes:
time: 1100 us; the launch traced here: 1080 us
  blocking collectives  536 us (49%)
  starting transfers between devices  198 us (18%)
  between operations  157 us (14%)
  local copies, waits for them, and re-layouts  77.4 us (7%)
  other arithmetic  56.5 us (5%)
  waiting for transfers between devices  39.4 us (4%)
  matrix products  15.8 us (1%)
    psum x3, blocking collectives, deflation_sums(): lax.psum((jnp.sum(residual * precond), project(images, precond)), ('gx',...  328 us
    psum x1, blocking collectives, per_device(): lax.psum((local_matrix, project(deflation, source)), ('gx', 'gy'))  105 us
    ppermute x30, starting transfers between devices, extended(): lax.ppermute(tail, axis, [(i, (i + 1) % count) for i in range(ends)])  104 us
    psum x1, blocking collectives, per_device(): alpha = inner_now / lax.psum(jnp.sum(search * image), ('gx', 'gy'))  103 us
    ppermute x30, starting transfers between devices, extended(): lax.ppermute(head, axis, [((i + 1) % count, i) for i in range(ends)])  86.7 us
    ppermute x30, waiting for transfers between devices, extended(): lax.ppermute(tail, axis, [(i, (i + 1) % count) for i in range(ends)])  38 us
    reduce_sum x39, other arithmetic, fold_pairs(): return values.reshape(new_shape).sum(axis=which + 1)  25.9 us
  transfers between devices with their start and end apart: 62, of which 29 were waited for; matrix products, arithmetic and copies ran while one was open for 5% of the time, Pallas kernels for 0%

commit v1 on v0

v1 whole, which is shorter than its diff:
```python
import functools

import jax
import jax.numpy as jnp
from jax import lax
from jax.experimental import pallas as pl
from jax.experimental.pallas import tpu as pltpu
from jax.sharding import PartitionSpec as P

LEVELS = 3
COARSE_SWEEPS = 3
ITERS = 2
BASIS = 8
RELAX_WEIGHT = 0.6

N = 16
LANES = 128
ROW = 4
SUMS = 2 * ITERS + 1
CYCLES = ITERS
FINE_EXCHANGES = 2 * CYCLES + ITERS
MID_EXCHANGES = 2 * CYCLES
COARSE_EXCHANGES = (COARSE_SWEEPS - 1) * CYCLES
EXCHANGES = (FINE_EXCHANGES, MID_EXCHANGES, COARSE_EXCHANGES)

FF, LF, FS, LS, FT, LT, DIAG, INV = range(8)


def kernel(
    sizes,
    source,
    diffuse_first,
    diffuse_second,
    diffuse_third,
    reaction,
    deflation,
    iterate_out,
    residual_out,
    level0,
    level1,
    level2,
    images,
    search,
    face_send,
    face_recv,
    basis_second_send,
    basis_first_recv,
    basis_second_recv,
    first_send0,
    first_recv0,
    second_send0,
    second_recv0,
    first_send1,
    first_recv1,
    second_send1,
    second_recv1,
    first_send2,
    first_recv2,
    second_send2,
    second_recv2,
    gather_second,
    gather_x,
    gather_y,
    setup_sems,
    halo_sems0,
    halo_sems1,
    halo_sems2,
    sum_sems,
):
    gx_count, gy_count = sizes
    x_count = ROW
    y_count = gx_count // ROW
    gx = lax.axis_index("gx")
    gy = lax.axis_index("gy")
    gx_next, gx_prev = lax.rem(gx + 1, gx_count), lax.rem(gx + gx_count - 1, gx_count)
    gy_next, gy_prev = lax.rem(gy + 1, gy_count), lax.rem(gy + gy_count - 1, gy_count)
    x, y = lax.rem(gx, x_count), gx // x_count

    second_peers = [(gx, lax.rem(gy + d, gy_count)) for d in range(1, gy_count)]
    x_peers = [(y * x_count + lax.rem(x + d, x_count), gy) for d in range(1, x_count)]
    y_peers = [(lax.rem(y + d, y_count) * x_count + x, gy) for d in range(1, y_count)]

    barrier = pltpu.get_barrier_semaphore()
    greeted = second_peers + x_peers + y_peers + [(gx_next, gy), (gx_prev, gy)]
    for peer in greeted:
        pl.semaphore_signal(
            barrier, inc=1, device_id=peer, device_id_type=pl.DeviceIdType.MESH
        )

    def send(src, dst, sems, peer):
        copy = pltpu.make_async_remote_copy(
            src_ref=src,
            dst_ref=dst,
            send_sem=sems[0],
            recv_sem=sems[1],
            device_id=peer,
            device_id_type=pl.DeviceIdType.MESH,
        )
        copy.start()
        return copy

    def iota(shape, dim):
        return lax.broadcasted_iota(jnp.int32, shape, dim)

    def roll(values, shift, axis):
        return pltpu.roll(values, shift, axis)

    levels = (level0, level1, level2)
    halo_refs = (
        (first_send0, first_recv0, second_send0, second_recv0, halo_sems0),
        (first_send1, first_recv1, second_send1, second_recv1, halo_sems1),
        (first_send2, first_recv2, second_send2, second_recv2, halo_sems2),
    )
    used = [0, 0, 0]

    shape = (N, N, LANES)
    last_first = (iota(shape, 0) == N - 1) & (gx == gx_count - 1)
    last_second = (iota(shape, 1) == N - 1) & (gy == gy_count - 1)
    last_third = iota(shape, 2) == LANES - 1
    face_first = jnp.where(last_first, 0.0, diffuse_first[...])
    face_second = jnp.where(last_second, 0.0, diffuse_second[...])
    face_third = jnp.where(last_third, 0.0, diffuse_third[...])
    level0[FF] = face_first
    level0[FS] = face_second
    level0[FT] = face_third
    level0[LT] = roll(face_third, 1, 2)
    face_send[0] = face_first[N - 1]
    face_send[1] = face_second[:, N - 1, :]
    basis = deflation[...]
    basis_second_send[0] = basis[:, :, 0, :]
    basis_second_send[1] = basis[:, :, N - 1, :]

    pl.semaphore_wait(barrier, len(greeted))

    def setup_pair(place):
        return setup_sems.at[0, place], setup_sems.at[1, place]

    setup_copies = [
        send(face_send.at[0], face_recv.at[0], setup_pair(0), (gx_next, gy)),
        send(face_send.at[1], face_recv.at[1], setup_pair(1), (gx, gy_next)),
        send(basis_second_send.at[0], basis_second_recv.at[1], setup_pair(2), (gx, gy_prev)),
        send(basis_second_send.at[1], basis_second_recv.at[0], setup_pair(3), (gx, gy_next)),
        send(deflation.at[:, 0], basis_first_recv.at[1], setup_pair(4), (gx_prev, gy)),
        send(deflation.at[:, N - 1], basis_first_recv.at[0], setup_pair(5), (gx_next, gy)),
    ]
    setup_copies[0].wait()
    setup_copies[1].wait()
    row0 = iota(shape, 1)
    lower_first = jnp.concatenate([face_recv[0][None], face_first[: N - 1]], axis=0)
    lower_second = jnp.where(row0 == 0, face_recv[1][:, None, :], roll(face_second, 1, 1))
    level0[LF] = lower_first
    level0[LS] = lower_second

    def finish_level(level, react):
        diag = react + level[FF] + level[LF] + level[FS] + level[LS] + level[FT] + level[LT]
        level[DIAG] = diag
        level[INV] = 1.0 / diag

    finish_level(level0, reaction[...])

    def partner_up(values, step, axis):
        return roll(values, values.shape[axis] - step, axis)

    def halves(values, step, axis):
        even = lax.rem(iota(values.shape, axis) // step, 2) == 0
        return (
            jnp.where(even, values, roll(values, step, axis)),
            jnp.where(even, partner_up(values, step, axis), values),
        )

    def fold(values, step, axis):
        if axis == 0:
            pairs = values.reshape((values.shape[0] // 2, 2) + values.shape[1:])
            return pairs[:, 0] + pairs[:, 1]
        even, odd = halves(values, step, axis)
        return even + odd

    def first_half(values, which):
        pairs = values.reshape((values.shape[0] // 2, 2) + values.shape[1:])
        return pairs[:, which]

    def fold_block(values, step):
        return fold(fold(fold(values, step, 0), step, 1), step, 2)

    def coarsen(fine, coarse, react, step):
        coarse[FF] = fold(fold(first_half(fine[FF], 1), step, 1), step, 2)
        coarse[LF] = fold(fold(first_half(fine[LF], 0), step, 1), step, 2)
        coarse[FS] = halves(fold(fold(fine[FS], step, 0), step, 2), step, 1)[1]
        coarse[LS] = halves(fold(fold(fine[LS], step, 0), step, 2), step, 1)[0]
        coarse[FT] = halves(fold(fold(fine[FT], step, 0), step, 1), step, 2)[1]
        coarse[LT] = halves(fold(fold(fine[LT], step, 0), step, 1), step, 2)[0]
        react = fold_block(react, step)
        finish_level(coarse, react)
        return react

    react1 = coarsen(level0, level1, reaction[...], 1)
    coarsen(level1, level2, react1, 2)

    def inner_part(field, level, step):
        return (
            level[DIAG] * field
            - level[FT] * partner_up(field, step, 2)
            - level[LT] * roll(field, step, 2)
        )

    def outer_part(partial, field, level, step, first_lo, first_hi, second_lo, second_hi):
        row = iota(field.shape, 1)
        upper = jnp.where(row >= N - step, second_hi[:, None, :], partner_up(field, step, 1))
        lower = jnp.where(row < step, second_lo[:, None, :], roll(field, step, 1))
        if field.shape[0] > 1:
            after = jnp.concatenate([field[1:], first_hi[None]], axis=0)
            before = jnp.concatenate([first_lo[None], field[:-1]], axis=0)
        return (
            partial
            - level[FF] * after
            - level[LF] * before
            - level[FS] * upper
            - level[LS] * lower
        )

    def operate(field, which):
        level = levels[which]
        step = 2**which
        first_send, first_recv, second_send, second_recv, sems = halo_refs[which]
        use = used[which]
        used[which] += 1
        cells = field.shape[0]
        first_send[use, 0] = field[0]
        first_send[use, 1] = field[cells - 1]
        second_send[use, 0] = field[:, 0, :]
        second_send[use, 1] = field[:, N - 1, :]

        def pair(place):
            return sems.at[0, use, place], sems.at[1, use, place]

        copies = [
            send(first_send.at[use, 0], first_recv.at[use, 1], pair(0), (gx_prev, gy)),
            send(first_send.at[use, 1], first_recv.at[use, 0], pair(1), (gx_next, gy)),
            send(second_send.at[use, 0], second_recv.at[use, 1], pair(2), (gx, gy_prev)),
            send(second_send.at[use, 1], second_recv.at[use, 0], pair(3), (gx, gy_next)),
        ]
        partial = inner_part(field, level, step)
        for copy in copies:
            copy.wait()
        return outer_part(
            partial,
            field,
            level,
            step,
            first_recv[use, 0],
            first_recv[use, 1],
            second_recv[use, 0],
            second_recv[use, 1],
        )

    def prolong_first(values):
        cells = values.shape[0]
        pairs = jnp.broadcast_to(values[:, None], (cells, 2) + values.shape[1:])
        return pairs.reshape((2 * cells,) + values.shape[1:])

    def cycle(right, which):
        level = levels[which]
        field = RELAX_WEIGHT * right * level[INV]
        if which == LEVELS - 1:
            for _ in range(COARSE_SWEEPS - 1):
                field = field + RELAX_WEIGHT * (right - operate(field, which)) * level[INV]
            return field
        defect = right - operate(field, which)
        field = field + prolong_first(cycle(fold_block(defect, 2**which), which + 1))
        return field + RELAX_WEIGHT * (right - operate(field, which)) * level[INV]

    summed = [0]

    def sum_devices(tile):
        use = summed[0]
        summed[0] += 1
        place = 0
        for buffer, peers, mine in (
            (gather_second, second_peers, gy),
            (gather_x, x_peers, x),
            (gather_y, y_peers, y),
        ):
            slot = buffer.at[use, mine]
            slot[...] = tile
            copies = []
            for peer in peers:
                sems = sum_sems.at[0, use, place], sum_sems.at[1, use, place]
                copies.append(send(slot, slot, sems, peer))
                place += 1
            for copy in copies:
                copy.wait()
            tile = jnp.sum(buffer[use], axis=0)
        return tile

    tile_shape = (8, LANES)
    lane = iota(tile_shape, 1)
    sub = iota(tile_shape, 0)

    def total(values):
        part = jnp.sum(values, axis=0)
        part = part[:8] + part[8:]
        part = jnp.sum(part, axis=0, keepdims=True)
        return jnp.broadcast_to(jnp.sum(part, axis=1, keepdims=True), tile_shape)

    def project(vectors, field):
        gathered = jnp.zeros(tile_shape, jnp.float32)
        for i in range(BASIS):
            part = jnp.sum(vectors[i] * field, axis=0)
            part = jnp.sum(part[:8] + part[8:], axis=0, keepdims=True)
            gathered = jnp.where(sub == i, part, gathered)
        return jnp.broadcast_to(jnp.sum(gathered, axis=1, keepdims=True), tile_shape)

    for copy in setup_copies[2:]:
        copy.wait()

    def image_step(j, tile):
        vector = deflation[j]
        image = outer_part(
            inner_part(vector, level0, 1),
            vector,
            level0,
            1,
            basis_first_recv[0, j],
            basis_first_recv[1, j],
            basis_second_recv[0, j],
            basis_second_recv[1, j],
        )
        images[j] = image
        return jnp.where(lane == j, project(deflation, image), tile)

    tile = lax.fori_loop(0, BASIS, image_step, jnp.zeros(tile_shape, jnp.float32))
    tile = jnp.where(lane == BASIS, project(deflation, source[...]), tile)
    tile = sum_devices(tile)

    def column(values, place):
        return jnp.sum(jnp.where(lane == place, values, 0.0), axis=1, keepdims=True)

    flipped = jnp.zeros(tile_shape, jnp.float32)
    for i in range(BASIS):
        col = column(tile, i)
        turned = jnp.sum(jnp.where(lane == sub, col, 0.0), axis=0, keepdims=True)
        flipped = jnp.where(sub == i, turned, flipped)
    projections = column(tile, BASIS)
    work = jnp.where(lane < BASIS, 0.5 * (tile + flipped), 0.0)
    work = jnp.where(lane - 2 * BASIS == sub, 1.0, work)
    for k in range(BASIS):
        col = column(work, k)
        pivot = col[k : k + 1]
        scaled = work[k : k + 1] / pivot
        work = jnp.where(sub == k, scaled, work - col * scaled)
    inverse_columns = [column(work, 2 * BASIS + i) for i in range(BASIS)]

    def solve(values):
        return [
            jnp.sum(
                jnp.broadcast_to(inverse_columns[i], tile_shape) * values,
                axis=0,
                keepdims=True,
            )[None]
            for i in range(BASIS)
        ]

    def expand(vectors, weights):
        out = weights[0] * vectors[0]
        for i in range(1, BASIS):
            out = out + weights[i] * vectors[i]
        return out

    weights = solve(jnp.broadcast_to(projections, tile_shape))
    iterate_out[...] = expand(deflation, weights)
    residual_out[...] = source[...] - expand(images, weights)

    def precondition():
        residual = residual_out[...]
        precond = cycle(residual, 0)
        sums = jnp.where(
            lane < 64, project(images, precond), total(residual * precond)
        )
        sums = sum_devices(sums)
        turned = roll(sums, 64, 1)
        inner = jnp.where(lane < 64, turned, sums)
        return precond, inner, solve(jnp.where(lane < 64, sums, turned))

    precond, inner_now, weights = precondition()
    search[...] = precond - expand(deflation, weights)
    for turn in range(ITERS):
        direction = search[...]
        image = operate(direction, 0)
        alpha = (inner_now / sum_devices(total(direction * image)))[:1][None]
        iterate_out[...] = iterate_out[...] + alpha * direction
        residual_out[...] = residual_out[...] - alpha * image
        if turn + 1 < ITERS:
            precond, inner_next, weights = precondition()
            ratio = (inner_next / inner_now)[:1][None]
            search[...] = precond + ratio * search[...] - expand(deflation, weights)
            inner_now = inner_next


def per_device(sizes, *args):
    gx_count, gy_count = sizes
    vmem = lambda *shape: pltpu.VMEM(shape, jnp.float32)
    scratch = [
        vmem(8, N, N, LANES),
        vmem(8, N // 2, N, LANES),
        vmem(8, N // 4, N, LANES),
        vmem(BASIS, N, N, LANES),
        vmem(N, N, LANES),
        vmem(2, N, LANES),
        vmem(2, N, LANES),
        vmem(2, BASIS, N, LANES),
        vmem(2, BASIS, N, LANES),
        vmem(2, BASIS, N, LANES),
    ]
    for which, count in enumerate(EXCHANGES):
        scratch += [vmem(count, 2, N, LANES)] * 2 + [vmem(count, 2, N // 2**which, LANES)] * 2
    peers = gy_count - 1 + ROW - 1 + gx_count // ROW - 1
    scratch += [
        vmem(SUMS, gy_count, 8, LANES),
        vmem(SUMS, ROW, 8, LANES),
        vmem(SUMS, gx_count // ROW, 8, LANES),
        pltpu.SemaphoreType.DMA((2, 6)),
        pltpu.SemaphoreType.DMA((2, FINE_EXCHANGES, 4)),
        pltpu.SemaphoreType.DMA((2, MID_EXCHANGES, 4)),
        pltpu.SemaphoreType.DMA((2, COARSE_EXCHANGES, 4)),
        pltpu.SemaphoreType.DMA((2, SUMS, peers)),
    ]
    block = jax.ShapeDtypeStruct((N, N, LANES), jnp.float32)
    return pl.pallas_call(
        functools.partial(kernel, sizes),
        out_shape=(block, block),
        in_specs=[pl.BlockSpec(memory_space=pltpu.VMEM)] * 6,
        out_specs=(pl.BlockSpec(memory_space=pltpu.VMEM),) * 2,
        scratch_shapes=scratch,
        compiler_params=pltpu.CompilerParams(
            collective_id=0, has_side_effects=True, vmem_limit_bytes=48 * 1024 * 1024
        ),
        name="deflated_cg",
    )(*args)


def solution(mesh):
    sizes = (mesh.shape["gx"], mesh.shape["gy"])
    field = P("gx", "gy", None)
    return jax.shard_map(
        functools.partial(per_device, sizes),
        mesh=mesh,
        in_specs=(field, field, field, field, field, P(None, "gx", "gy", None)),
        out_specs=(field, field),
        check_vma=False,
    )
```

time: 1100 us -> 157 us (0.14)
  the two profiles are of different devices: /device:TPU:27 before, /device:TPU:8 now
where the time goes in v1:
time: 157 us
  Pallas kernels  149 us (95%)
  local copies, waits for them, and re-layouts  7.05 us (4%)
    pallas_call x1, Pallas kernels, per_device(): pl.pallas_call(functools.partial(kernel, sizes), out_shape=(block, block)...  149 us
    unnamed x14, local copies, waits for them, and re-layouts  7.05 us

profile of v1, /device:TPU:8, one launch (start us, length us, event | category | flops | bytes accessed | tf_op | source)
XLA Modules:
  0.0 157.2 jit_solution(17349768638671629447)
XLA Ops:
  0.6 0.0 copy-start
  0.6 1.2 copy-done
  1.9 0.0 copy-start.1
  1.9 0.9 copy-done.1
  2.8 0.0 copy-start.2
  2.8 0.9 copy-done.2
  3.7 0.0 copy-start.3
  3.7 0.9 copy-done.3
  4.6 0.0 copy-start.4
  4.6 0.9 copy-done.4
  5.5 0.0 copy-start.5
  5.5 0.9 copy-done.5
  6.4 149.5 %deflated_cg.1 = (f32[16,16,128]{2,1,0:T(8,128)S(1)}, f32[16,16,128]{2,1,0:T(8,128)S(1)}) custom-call(f32[16,16,128]{2,1,0:T(8,128)S(1)} %copy-done.1, f32[16,16,128]{2,1,0:T(8,128)S(1)} %copy-done.2, f32[16,16,128]{2,1,0:T(8,128)S(1)} %copy-done.3, f32[16,16,128]{2,1,0:T(8,128)S(1)} %copy-done.4, f32[16,16,128]{2,1,0:T(8,128)S(1)} %copy-done.5, ...), custom_call_target="tpu_custom_call" | custom-call | tf_op jit(solution)/shard_map/deflated_cg/pallas_call | solution.py:428
  155.8 0.7 copy.10
  156.5 0.7 copy.11
Async XLA Ops:
  0.6 1.2 copy-start
  1.9 0.9 copy-start.1
  2.8 0.9 copy-start.2
  3.7 0.9 copy-start.3
  4.6 0.9 copy-start.4
  5.5 0.9 copy-start.5

commit v2 on v1

--- a/solution.py
+++ b/solution.py
@@ -15,8 +15,7 @@
 
 N = 16
 LANES = 128
-ROW = 4
-SUMS = 2 * ITERS + 1
+SUMS = ITERS + 1
 CYCLES = ITERS
 FINE_EXCHANGES = 2 * CYCLES + ITERS
 MID_EXCHANGES = 2 * CYCLES
@@ -41,6 +40,7 @@
     level2,
     images,
     search,
+    image_kept,
     face_send,
     face_recv,
     basis_second_send,
@@ -59,8 +59,7 @@
     second_send2,
     second_recv2,
     gather_second,
-    gather_x,
-    gather_y,
+    gather_first,
     setup_sems,
     halo_sems0,
     halo_sems1,
@@ -68,20 +67,16 @@
     sum_sems,
 ):
     gx_count, gy_count = sizes
-    x_count = ROW
-    y_count = gx_count // ROW
     gx = lax.axis_index("gx")
     gy = lax.axis_index("gy")
     gx_next, gx_prev = lax.rem(gx + 1, gx_count), lax.rem(gx + gx_count - 1, gx_count)
     gy_next, gy_prev = lax.rem(gy + 1, gy_count), lax.rem(gy + gy_count - 1, gy_count)
-    x, y = lax.rem(gx, x_count), gx // x_count
 
     second_peers = [(gx, lax.rem(gy + d, gy_count)) for d in range(1, gy_count)]
-    x_peers = [(y * x_count + lax.rem(x + d, x_count), gy) for d in range(1, x_count)]
-    y_peers = [(lax.rem(y + d, y_count) * x_count + x, gy) for d in range(1, y_count)]
+    first_peers = [(lax.rem(gx + d, gx_count), gy) for d in range(1, gx_count)]
 
     barrier = pltpu.get_barrier_semaphore()
-    greeted = second_peers + x_peers + y_peers + [(gx_next, gy), (gx_prev, gy)]
+    greeted = second_peers + first_peers
     for peer in greeted:
         pl.semaphore_signal(
             barrier, inc=1, device_id=peer, device_id_type=pl.DeviceIdType.MESH
@@ -218,7 +213,7 @@
             - level[LS] * lower
         )
 
-    def operate(field, which):
+    def operate(field, which, meanwhile=lambda: None):
         level = levels[which]
         step = 2**which
         first_send, first_recv, second_send, second_recv, sems = halo_refs[which]
@@ -240,6 +235,7 @@
             send(second_send.at[use, 1], second_recv.at[use, 0], pair(3), (gx, gy_next)),
         ]
         partial = inner_part(field, level, step)
+        meanwhile()
         for copy in copies:
             copy.wait()
         return outer_part(
@@ -271,17 +267,16 @@
 
     summed = [0]
 
-    def sum_devices(tile):
+    def sum_devices(row):
         use = summed[0]
         summed[0] += 1
         place = 0
         for buffer, peers, mine in (
             (gather_second, second_peers, gy),
-            (gather_x, x_peers, x),
-            (gather_y, y_peers, y),
+            (gather_first, first_peers, gx),
         ):
             slot = buffer.at[use, mine]
-            slot[...] = tile
+            slot[...] = row
             copies = []
             for peer in peers:
                 sems = sum_sems.at[0, use, place], sum_sems.at[1, use, place]
@@ -289,26 +284,26 @@
                 place += 1
             for copy in copies:
                 copy.wait()
-            tile = jnp.sum(buffer[use], axis=0)
-        return tile
+            row = jnp.sum(buffer[use], axis=0)
+        return row
 
     tile_shape = (8, LANES)
     lane = iota(tile_shape, 1)
     sub = iota(tile_shape, 0)
 
-    def total(values):
-        part = jnp.sum(values, axis=0)
-        part = part[:8] + part[8:]
-        part = jnp.sum(part, axis=0, keepdims=True)
-        return jnp.broadcast_to(jnp.sum(part, axis=1, keepdims=True), tile_shape)
-
-    def project(vectors, field):
+    def parts(fields):
         gathered = jnp.zeros(tile_shape, jnp.float32)
-        for i in range(BASIS):
-            part = jnp.sum(vectors[i] * field, axis=0)
+        for i, field in enumerate(fields):
+            part = jnp.sum(field, axis=0)
             part = jnp.sum(part[:8] + part[8:], axis=0, keepdims=True)
             gathered = jnp.where(sub == i, part, gathered)
-        return jnp.broadcast_to(jnp.sum(gathered, axis=1, keepdims=True), tile_shape)
+        return jnp.sum(gathered, axis=1, keepdims=True)
+
+    def project(vectors, field):
+        return parts(vectors[i] * field for i in range(BASIS))
+
+    def pick(row, places):
+        return jnp.sum(jnp.where(lane == places, row, 0.0), axis=1, keepdims=True)
 
     for copy in setup_copies[2:]:
         copy.wait()
@@ -326,23 +321,22 @@
             basis_second_recv[1, j],
         )
         images[j] = image
-        return jnp.where(lane == j, project(deflation, image), tile)
+        return jnp.where(lane == j * BASIS + sub, project(deflation, image), tile)
 
     tile = lax.fori_loop(0, BASIS, image_step, jnp.zeros(tile_shape, jnp.float32))
-    tile = jnp.where(lane == BASIS, project(deflation, source[...]), tile)
-    tile = sum_devices(tile)
+    tile = jnp.where(
+        lane == BASIS * BASIS + sub, project(deflation, source[...]), tile
+    )
+    row = sum_devices(jnp.sum(tile, axis=0, keepdims=True))
 
     def column(values, place):
         return jnp.sum(jnp.where(lane == place, values, 0.0), axis=1, keepdims=True)
 
-    flipped = jnp.zeros(tile_shape, jnp.float32)
-    for i in range(BASIS):
-        col = column(tile, i)
-        turned = jnp.sum(jnp.where(lane == sub, col, 0.0), axis=0, keepdims=True)
-        flipped = jnp.where(sub == i, turned, flipped)
-    projections = column(tile, BASIS)
-    work = jnp.where(lane < BASIS, 0.5 * (tile + flipped), 0.0)
-    work = jnp.where(lane - 2 * BASIS == sub, 1.0, work)
+    projections = pick(row, BASIS * BASIS + sub)
+    work = jnp.where(lane - 2 * BASIS == sub, 1.0, 0.0)
+    for j in range(BASIS):
+        both = 0.5 * (pick(row, BASIS * j + sub) + pick(row, BASIS * sub + j))
+        work = jnp.where(lane == j, both, work)
     for k in range(BASIS):
         col = column(work, k)
         pivot = col[k : k + 1]
@@ -370,30 +364,44 @@
     iterate_out[...] = expand(deflation, weights)
     residual_out[...] = source[...] - expand(images, weights)
 
-    def precondition():
+    inner_now = curve = None
+    for turn in range(ITERS):
         residual = residual_out[...]
         precond = cycle(residual, 0)
-        sums = jnp.where(
-            lane < 64, project(images, precond), total(residual * precond)
-        )
-        sums = sum_devices(sums)
-        turned = roll(sums, 64, 1)
-        inner = jnp.where(lane < 64, turned, sums)
-        return precond, inner, solve(jnp.where(lane < 64, sums, turned))
-
-    precond, inner_now, weights = precondition()
-    search[...] = precond - expand(deflation, weights)
-    for turn in range(ITERS):
-        direction = search[...]
-        image = operate(direction, 0)
-        alpha = (inner_now / sum_devices(total(direction * image)))[:1][None]
+        held = []
+
+        def products():
+            held.append(project(images, precond))
+            held.append(residual * precond)
+            if turn > 0:
+                held.append(precond * image_kept[...])
+
+        image = operate(precond, 0, products)
+        scalars = parts([precond * image] + held[1:])
+        tile = jnp.where(lane == sub, held[0], 0.0)
+        tile = jnp.where(lane == BASIS + sub, scalars, tile)
+        row = sum_devices(jnp.sum(tile, axis=0, keepdims=True))
+        projected = jnp.broadcast_to(pick(row, sub), tile_shape)
+        curve_next, inner_next, cross = [
+            jnp.broadcast_to(pick(row, BASIS + i)[:1], (1, LANES))[None] for i in range(3)
+        ]
+        weights = solve(projected)
+        for i in range(BASIS):
+            curve_next = curve_next - weights[i] * projected[i : i + 1][None]
+        direction = precond - expand(deflation, weights)
+        image = image - expand(images, weights)
+        if turn > 0:
+            ratio = inner_next / inner_now
+            direction = direction + ratio * search[...]
+            image = image + ratio * image_kept[...]
+            curve_next = curve_next + ratio * (ratio * curve + 2.0 * cross)
+        inner_now, curve = inner_next, curve_next
+        alpha = inner_now / curve
         iterate_out[...] = iterate_out[...] + alpha * direction
         residual_out[...] = residual_out[...] - alpha * image
         if turn + 1 < ITERS:
-            precond, inner_next, weights = precondition()
-            ratio = (inner_next / inner_now)[:1][None]
-            search[...] = precond + ratio * search[...] - expand(deflation, weights)
-            inner_now = inner_next
+            search[...] = direction
+            image_kept[...] = image
 
 
 def per_device(sizes, *args):
@@ -405,6 +413,7 @@
         vmem(8, N // 4, N, LANES),
         vmem(BASIS, N, N, LANES),
         vmem(N, N, LANES),
+        vmem(N, N, LANES),
         vmem(2, N, LANES),
         vmem(2, N, LANES),
         vmem(2, BASIS, N, LANES),
@@ -413,11 +422,10 @@
     ]
     for which, count in enumerate(EXCHANGES):
         scratch += [vmem(count, 2, N, LANES)] * 2 + [vmem(count, 2, N // 2**which, LANES)] * 2
-    peers = gy_count - 1 + ROW - 1 + gx_count // ROW - 1
+    peers = gy_count - 1 + gx_count - 1
     scratch += [
-        vmem(SUMS, gy_count, 8, LANES),
-        vmem(SUMS, ROW, 8, LANES),
-        vmem(SUMS, gx_count // ROW, 8, LANES),
+        vmem(SUMS, gy_count, 1, LANES),
+        vmem(SUMS, gx_count, 1, LANES),
         pltpu.SemaphoreType.DMA((2, 6)),
         pltpu.SemaphoreType.DMA((2, FINE_EXCHANGES, 4)),
         pltpu.SemaphoreType.DMA((2, MID_EXCHANGES, 4)),

time: 157 us -> 125 us (0.80)
  the two profiles are of different devices: /device:TPU:8 before, /device:TPU:2 now
where the time goes in v2:
time: 125 us
  Pallas kernels  117 us (94%)
  local copies, waits for them, and re-layouts  7.05 us (6%)
    pallas_call x1, Pallas kernels, per_device(): pl.pallas_call(functools.partial(kernel, sizes), out_shape=(block, block)...  117 us
    unnamed x14, local copies, waits for them, and re-layouts  7.05 us

profile of v2, /device:TPU:2, one launch (start us, length us, event | category | flops | bytes accessed | tf_op | source)
XLA Modules:
  0.0 125.2 jit_solution(17167874896411112069)
XLA Ops:
  0.6 0.0 copy-start
  0.6 1.2 copy-done
  1.9 0.0 copy-start.1
  1.9 0.9 copy-done.1
  2.8 0.0 copy-start.2
  2.8 0.9 copy-done.2
  3.7 0.0 copy-start.3
  3.7 0.9 copy-done.3
  4.6 0.0 copy-start.4
  4.6 0.9 copy-done.4
  5.5 0.0 copy-start.5
  5.5 0.9 copy-done.5
  6.4 117.5 %deflated_cg.1 = (f32[16,16,128]{2,1,0:T(8,128)S(1)}, f32[16,16,128]{2,1,0:T(8,128)S(1)}) custom-call(f32[16,16,128]{2,1,0:T(8,128)S(1)} %copy-done.1, f32[16,16,128]{2,1,0:T(8,128)S(1)} %copy-done.2, f32[16,16,128]{2,1,0:T(8,128)S(1)} %copy-done.3, f32[16,16,128]{2,1,0:T(8,128)S(1)} %copy-done.4, f32[16,16,128]{2,1,0:T(8,128)S(1)} %copy-done.5, ...), custom_call_target="tpu_custom_call" | custom-call | tf_op jit(solution)/shard_map/deflated_cg/pallas_call | solution.py:436
  123.9 0.7 copy.10
  124.5 0.7 copy.11
Async XLA Ops:
  0.6 1.2 copy-start
  1.9 0.9 copy-start.1
  2.8 0.9 copy-start.2
  3.7 0.9 copy-start.3
  4.6 0.9 copy-start.4
  5.5 0.9 copy-start.5

commit v3 on v2

--- a/solution.py
+++ b/solution.py
@@ -213,6 +213,21 @@
             - level[LS] * lower
         )
 
+    mate_first = gx + 1 - 2 * lax.rem(gx, 2)
+    mate_second = gy + 1 - 2 * lax.rem(gy, 2)
+    starts, ends = gx == 0, gx == gx_count - 1
+    opens, closes = gy == 0, gy == gy_count - 1
+    peers = (
+        (jnp.where(starts, gx, gx_prev), jnp.where(starts, mate_second, gy)),
+        (jnp.where(ends, gx, gx_next), jnp.where(ends, mate_second, gy)),
+        (jnp.where(opens, mate_first, gx), jnp.where(opens, gy, gy_prev)),
+        (jnp.where(closes, mate_first, gx), jnp.where(closes, gy, gy_next)),
+    )
+    slots = tuple(
+        jnp.where(at, other, slot).astype(jnp.int32)
+        for at, other, slot in ((starts, 0, 1), (ends, 1, 0), (opens, 0, 1), (closes, 1, 0))
+    )
+
     def operate(field, which, meanwhile=lambda: None):
         level = levels[which]
         step = 2**which
@@ -228,16 +243,33 @@
         def pair(place):
             return sems.at[0, use, place], sems.at[1, use, place]
 
-        copies = [
-            send(first_send.at[use, 0], first_recv.at[use, 1], pair(0), (gx_prev, gy)),
-            send(first_send.at[use, 1], first_recv.at[use, 0], pair(1), (gx_next, gy)),
-            send(second_send.at[use, 0], second_recv.at[use, 1], pair(2), (gx, gy_prev)),
-            send(second_send.at[use, 1], second_recv.at[use, 0], pair(3), (gx, gy_next)),
-        ]
+        copies = []
+        for place, (edge, slot, peer) in enumerate(
+            (
+                (first_send.at[use, 0], slots[0], peers[0]),
+                (first_send.at[use, 1], slots[1], peers[1]),
+                (second_send.at[use, 0], slots[2], peers[2]),
+                (second_send.at[use, 1], slots[3], peers[3]),
+            )
+        ):
+            first = place < 2
+            landing = (first_recv if first else second_recv).at[use, slot]
+            arrival = slot if first else slot + 2
+            pair = sems.at[0, use, place], sems.at[1, use, arrival]
+            copies.append(send(edge, landing, pair, peer))
         partial = inner_part(field, level, step)
         meanwhile()
-        for copy in copies:
-            copy.wait()
+        for place in range(4):
+            copies[place].wait_send()
+            landing = (first_recv if place < 2 else second_recv).at[use, place % 2]
+            pltpu.make_async_remote_copy(
+                src_ref=landing,
+                dst_ref=landing,
+                send_sem=sems.at[0, use, place],
+                recv_sem=sems.at[1, use, place],
+                device_id=peers[place],
+                device_id_type=pl.DeviceIdType.MESH,
+            ).wait_recv()
         return outer_part(
             partial,
             field,

time: 125 us -> 125 us (level)
  no operation moved by 1% of the time
where the time goes in v3:
time: 125 us
  Pallas kernels  117 us (94%)
  local copies, waits for them, and re-layouts  7.05 us (6%)
    pallas_call x1, Pallas kernels, per_device(): pl.pallas_call(functools.partial(kernel, sizes), out_shape=(block, block)...  117 us
    unnamed x14, local copies, waits for them, and re-layouts  7.05 us

profile of v3, /device:TPU:2, one launch (start us, length us, event | category | flops | bytes accessed | tf_op | source)
XLA Modules:
  0.0 125.2 jit_solution(13168587190996349693)
XLA Ops:
  0.6 0.0 copy-start
  0.6 1.2 copy-done
  1.9 0.0 copy-start.1
  1.9 0.9 copy-done.1
  2.8 0.0 copy-start.2
  2.8 0.9 copy-done.2
  3.7 0.0 copy-start.3
  3.7 0.9 copy-done.3
  4.6 0.0 copy-start.4
  4.6 0.9 copy-done.4
  5.5 0.0 copy-start.5
  5.5 0.9 copy-done.5
  6.4 117.5 %deflated_cg.1 = (f32[16,16,128]{2,1,0:T(8,128)S(1)}, f32[16,16,128]{2,1,0:T(8,128)S(1)}) custom-call(f32[16,16,128]{2,1,0:T(8,128)S(1)} %copy-done.1, f32[16,16,128]{2,1,0:T(8,128)S(1)} %copy-done.2, f32[16,16,128]{2,1,0:T(8,128)S(1)} %copy-done.3, f32[16,16,128]{2,1,0:T(8,128)S(1)} %copy-done.4, f32[16,16,128]{2,1,0:T(8,128)S(1)} %copy-done.5, ...), custom_call_target="tpu_custom_call" | custom-call | tf_op jit(solution)/shard_map/deflated_cg/pallas_call | solution.py:468
  123.9 0.7 copy.10
  124.5 0.7 copy.11
Async XLA Ops:
  0.6 1.2 copy-start
  1.9 0.9 copy-start.1
  2.8 0.9 copy-start.2
  3.7 0.9 copy-start.3
  4.6 0.9 copy-start.4
  5.5 0.9 copy-start.5

commit v4 on v2

--- a/solution.py
+++ b/solution.py
@@ -149,7 +149,6 @@
     def finish_level(level, react):
         diag = react + level[FF] + level[LF] + level[FS] + level[LS] + level[FT] + level[LT]
         level[DIAG] = diag
-        level[INV] = 1.0 / diag
 
     finish_level(level0, reaction[...])
 
@@ -188,30 +187,42 @@
         finish_level(coarse, react)
         return react
 
-    react1 = coarsen(level0, level1, reaction[...], 1)
-    coarsen(level1, level2, react1, 2)
+    def coarsen_fine():
+        level0[INV] = 1.0 / level0[DIAG]
+        kept.append(coarsen(level0, level1, reaction[...], 1))
+
+    def coarsen_mid():
+        level1[INV] = 1.0 / level1[DIAG]
+        coarsen(level1, level2, kept[0], 2)
+        level2[INV] = 1.0 / level2[DIAG]
+
+    kept = []
 
     def inner_part(field, level, step):
+        row = iota(field.shape, 1)
+        upper = jnp.where(row >= N - step, 0.0, partner_up(field, step, 1))
+        lower = jnp.where(row < step, 0.0, roll(field, step, 1))
+        nothing = jnp.zeros_like(field[:1])
         return (
             level[DIAG] * field
             - level[FT] * partner_up(field, step, 2)
             - level[LT] * roll(field, step, 2)
-        )
-
-    def outer_part(partial, field, level, step, first_lo, first_hi, second_lo, second_hi):
-        row = iota(field.shape, 1)
-        upper = jnp.where(row >= N - step, second_hi[:, None, :], partner_up(field, step, 1))
-        lower = jnp.where(row < step, second_lo[:, None, :], roll(field, step, 1))
-        if field.shape[0] > 1:
-            after = jnp.concatenate([field[1:], first_hi[None]], axis=0)
-            before = jnp.concatenate([first_lo[None], field[:-1]], axis=0)
-        return (
-            partial
-            - level[FF] * after
-            - level[LF] * before
             - level[FS] * upper
             - level[LS] * lower
-        )
+            - level[FF] * jnp.concatenate([field[1:], nothing], axis=0)
+            - level[LF] * jnp.concatenate([nothing, field[:-1]], axis=0)
+        )
+
+    def outer_part(partial, level, step, first_lo, first_hi, second_lo, second_hi):
+        cells = partial.shape[0]
+        row = iota((cells, 8, LANES), 1)
+        low, high = level[LS, :, :8], level[FS, :, 8:]
+        low = jnp.where(row < step, low * second_lo[:, None, :], 0.0)
+        high = jnp.where(row >= 8 - step, high * second_hi[:, None, :], 0.0)
+        partial = jnp.concatenate([partial[:, :8] - low, partial[:, 8:] - high], axis=1)
+        front = partial[0] - level[LF, 0] * first_lo
+        back = partial[cells - 1] - level[FF, cells - 1] * first_hi
+        return jnp.concatenate([front[None], partial[1 : cells - 1], back[None]], axis=0)
 
     def operate(field, which, meanwhile=lambda: None):
         level = levels[which]
@@ -240,7 +251,6 @@
             copy.wait()
         return outer_part(
             partial,
-            field,
             level,
             step,
             first_recv[use, 0],
@@ -267,13 +277,13 @@
 
     summed = [0]
 
-    def sum_devices(row):
+    def sum_devices(row, meanwhile=(lambda: None, lambda: None)):
         use = summed[0]
         summed[0] += 1
         place = 0
-        for buffer, peers, mine in (
-            (gather_second, second_peers, gy),
-            (gather_first, first_peers, gx),
+        for buffer, peers, mine, work in (
+            (gather_second, second_peers, gy, meanwhile[0]),
+            (gather_first, first_peers, gx, meanwhile[1]),
         ):
             slot = buffer.at[use, mine]
             slot[...] = row
@@ -282,6 +292,7 @@
                 sems = sum_sems.at[0, use, place], sum_sems.at[1, use, place]
                 copies.append(send(slot, slot, sems, peer))
                 place += 1
+            work()
             for copy in copies:
                 copy.wait()
             row = jnp.sum(buffer[use], axis=0)
@@ -305,6 +316,7 @@
     def pick(row, places):
         return jnp.sum(jnp.where(lane == places, row, 0.0), axis=1, keepdims=True)
 
+    source_parts = project(deflation, source[...])
     for copy in setup_copies[2:]:
         copy.wait()
 
@@ -312,7 +324,6 @@
         vector = deflation[j]
         image = outer_part(
             inner_part(vector, level0, 1),
-            vector,
             level0,
             1,
             basis_first_recv[0, j],
@@ -324,10 +335,8 @@
         return jnp.where(lane == j * BASIS + sub, project(deflation, image), tile)
 
     tile = lax.fori_loop(0, BASIS, image_step, jnp.zeros(tile_shape, jnp.float32))
-    tile = jnp.where(
-        lane == BASIS * BASIS + sub, project(deflation, source[...]), tile
-    )
-    row = sum_devices(jnp.sum(tile, axis=0, keepdims=True))
+    tile = jnp.where(lane == BASIS * BASIS + sub, source_parts, tile)
+    row = sum_devices(jnp.sum(tile, axis=0, keepdims=True), (coarsen_fine, coarsen_mid))
 
     def column(values, place):
         return jnp.sum(jnp.where(lane == place, values, 0.0), axis=1, keepdims=True)

time: 125 us -> 125 us (level)
  no operation moved by 1% of the time
where the time goes in v4:
time: 125 us
  Pallas kernels  117 us (94%)
  local copies, waits for them, and re-layouts  7.05 us (6%)
    pallas_call x1, Pallas kernels, per_device(): pl.pallas_call(functools.partial(kernel, sizes), out_shape=(block, block)...  117 us
    unnamed x14, local copies, waits for them, and re-layouts  7.05 us

profile of v4, /device:TPU:2, one launch (start us, length us, event | category | flops | bytes accessed | tf_op | source)
XLA Modules:
  0.0 124.7 jit_solution(17901796339179466552)
XLA Ops:
  0.6 0.0 copy-start
  0.6 1.2 copy-done
  1.9 0.0 copy-start.1
  1.9 0.9 copy-done.1
  2.8 0.0 copy-start.2
  2.8 0.9 copy-done.2
  3.7 0.0 copy-start.3
  3.7 0.9 copy-done.3
  4.6 0.0 copy-start.4
  4.6 0.9 copy-done.4
  5.5 0.0 copy-start.5
  5.5 0.9 copy-done.5
  6.4 116.9 %deflated_cg.1 = (f32[16,16,128]{2,1,0:T(8,128)S(1)}, f32[16,16,128]{2,1,0:T(8,128)S(1)}) custom-call(f32[16,16,128]{2,1,0:T(8,128)S(1)} %copy-done.1, f32[16,16,128]{2,1,0:T(8,128)S(1)} %copy-done.2, f32[16,16,128]{2,1,0:T(8,128)S(1)} %copy-done.3, f32[16,16,128]{2,1,0:T(8,128)S(1)} %copy-done.4, f32[16,16,128]{2,1,0:T(8,128)S(1)} %copy-done.5, ...), custom_call_target="tpu_custom_call" | custom-call | tf_op jit(solution)/shard_map/deflated_cg/pallas_call | solution.py:445
  123.3 0.7 copy.10
  124.0 0.7 copy.11
Async XLA Ops:
  0.6 1.2 copy-start
  1.9 0.9 copy-start.1
  2.8 0.9 copy-start.2
  3.7 0.9 copy-start.3
  4.6 0.9 copy-start.4
  5.5 0.9 copy-start.5

commit v5 on v4

--- a/solution.py
+++ b/solution.py
@@ -82,6 +82,8 @@
             barrier, inc=1, device_id=peer, device_id_type=pl.DeviceIdType.MESH
         )
 
+    sent = []
+
     def send(src, dst, sems, peer):
         copy = pltpu.make_async_remote_copy(
             src_ref=src,
@@ -92,6 +94,7 @@
             device_id_type=pl.DeviceIdType.MESH,
         )
         copy.start()
+        sent.append(copy)
         return copy
 
     def iota(shape, dim):
@@ -138,8 +141,8 @@
         send(deflation.at[:, 0], basis_first_recv.at[1], setup_pair(4), (gx_prev, gy)),
         send(deflation.at[:, N - 1], basis_first_recv.at[0], setup_pair(5), (gx_next, gy)),
     ]
-    setup_copies[0].wait()
-    setup_copies[1].wait()
+    setup_copies[0].wait_recv()
+    setup_copies[1].wait_recv()
     row0 = iota(shape, 1)
     lower_first = jnp.concatenate([face_recv[0][None], face_first[: N - 1]], axis=0)
     lower_second = jnp.where(row0 == 0, face_recv[1][:, None, :], roll(face_second, 1, 1))
@@ -248,7 +251,7 @@
         partial = inner_part(field, level, step)
         meanwhile()
         for copy in copies:
-            copy.wait()
+            copy.wait_recv()
         return outer_part(
             partial,
             level,
@@ -294,7 +297,7 @@
                 place += 1
             work()
             for copy in copies:
-                copy.wait()
+                copy.wait_recv()
             row = jnp.sum(buffer[use], axis=0)
         return row
 
@@ -318,7 +321,7 @@
 
     source_parts = project(deflation, source[...])
     for copy in setup_copies[2:]:
-        copy.wait()
+        copy.wait_recv()
 
     def image_step(j, tile):
         vector = deflation[j]
@@ -411,6 +414,9 @@
         if turn + 1 < ITERS:
             search[...] = direction
             image_kept[...] = image
+
+    for copy in sent:
+        copy.wait_send()
 
 
 def per_device(sizes, *args):

time: 125 us -> 125 us (level)
  no operation moved by 1% of the time
where the time goes in v5:
time: 125 us
  Pallas kernels  117 us (94%)
  local copies, waits for them, and re-layouts  7.05 us (6%)
    pallas_call x1, Pallas kernels, per_device(): pl.pallas_call(functools.partial(kernel, sizes), out_shape=(block, block)...  117 us
    unnamed x14, local copies, waits for them, and re-layouts  7.05 us

profile of v5, /device:TPU:2, one launch (start us, length us, event | category | flops | bytes accessed | tf_op | source)
XLA Modules:
  0.0 124.8 jit_solution(13356635742533103240)
XLA Ops:
  0.6 0.0 copy-start
  0.6 1.2 copy-done
  1.9 0.0 copy-start.1
  1.9 0.9 copy-done.1
  2.8 0.0 copy-start.2
  2.8 0.9 copy-done.2
  3.7 0.0 copy-start.3
  3.7 0.9 copy-done.3
  4.6 0.0 copy-start.4
  4.6 0.9 copy-done.4
  5.5 0.0 copy-start.5
  5.5 0.9 copy-done.5
  6.4 117.1 %deflated_cg.1 = (f32[16,16,128]{2,1,0:T(8,128)S(1)}, f32[16,16,128]{2,1,0:T(8,128)S(1)}) custom-call(f32[16,16,128]{2,1,0:T(8,128)S(1)} %copy-done.1, f32[16,16,128]{2,1,0:T(8,128)S(1)} %copy-done.2, f32[16,16,128]{2,1,0:T(8,128)S(1)} %copy-done.3, f32[16,16,128]{2,1,0:T(8,128)S(1)} %copy-done.4, f32[16,16,128]{2,1,0:T(8,128)S(1)} %copy-done.5, ...), custom_call_target="tpu_custom_call" | custom-call | tf_op jit(solution)/shard_map/deflated_cg/pallas_call | solution.py:451
  123.5 0.7 copy.10
  124.2 0.7 copy.11
Async XLA Ops:
  0.6 1.2 copy-start
  1.9 0.9 copy-start.1
  2.8 0.9 copy-start.2
  3.7 0.9 copy-start.3
  4.6 0.9 copy-start.4
  5.5 0.9 copy-start.5
